TPU v7x, 768 devices: a whole 4x8x12 slice. The times are simulated.
768 devices in a mesh: section: 4 (over x), dp: 16 (over y, z_hi), tensor: 12 (over z_lo, core).
Axes of the slice: x: 4, y: 8, z: 12 (z_hi: 2, z_lo: 6; z = z_hi * 6 + z_lo), core: 2. Of those that a mesh axis runs over, the one named last changes fastest.
Arguments:
- enc_hidden: bfloat16 [16, 1152, 4096], P('dp', 'section'), may hold values from -6 to 6
- dec_hidden: bfloat16 [4, 16, 192, 4096], P('section', 'dp', 'tensor'), may hold values from -6 to 6
- enc_gain: bfloat16 [4096], replicated, may hold values from 0.25 to 1.75
- dec_gain: bfloat16 [4, 4096], P('section'), may hold values from 0.25 to 1.75
- w_query: bfloat16 [4, 4096, 3072], P('section', None, 'tensor'), may hold values from -0.0234375 to 0.0234375
- w_key: bfloat16 [4, 4096, 3072], P('section', None, 'tensor'), may hold values from -0.09375 to 0.09375
- w_value: bfloat16 [4, 4096, 3072], P('section', None, 'tensor'), may hold values from -0.09375 to 0.09375
- w_out: bfloat16 [4, 3072, 4096], P('section', 'tensor'), may hold values from -0.109375 to 0.109375
Outputs:
- cross_out: bfloat16 [4, 16, 192, 4096], P('section', 'dp', 'tensor')
All inputs are finite; a program needn't handle non-finite values.
Results may differ from a plain program's by a relative error of at most 0.017.
Values may be sent and summed in bfloat16 or wider, within the bound.
A program may use at most 64 MiB of HBM per device.

v0:
```python
import jax
import jax.numpy as jnp
from jax import lax
from jax.sharding import PartitionSpec as P

HD = 256


def normalize(hidden, gain):
    values = hidden.astype(jnp.float32)
    mean_sq = jnp.mean(values * values, axis=-1, keepdims=True)
    return (values * lax.rsqrt(mean_sq + 1e-06) * gain.astype(jnp.float32)).astype(jnp.bfloat16)


def body(enc_hidden, dec_hidden, enc_gain, dec_gain, w_query, w_key, w_value, w_out):
    memory = normalize(enc_hidden[0], enc_gain)
    normed = normalize(dec_hidden[0, 0], dec_gain[0])
    kv_weight = jnp.concatenate([w_key[0], w_value[0]], axis=1)
    width = w_key.shape[2]
    share_rows = memory.shape[0] // lax.axis_size("tensor")
    own_share = lax.dynamic_slice_in_dim(
        memory, lax.axis_index("tensor") * share_rows, share_rows, 0
    )
    projected = jnp.dot(
        lax.all_gather(own_share, ("section", "tensor"), axis=0, tiled=True),
        kv_weight,
        preferred_element_type=jnp.float32,
    ).astype(jnp.bfloat16)
    keys = projected[:, :width].reshape(projected.shape[0], -1, HD)
    values = projected[:, width:].reshape(projected.shape[0], -1, HD)
    queries = jnp.dot(
        lax.all_gather(normed, "tensor", axis=0, tiled=True),
        w_query[0],
        preferred_element_type=jnp.float32,
    ).astype(jnp.bfloat16)
    queries = queries.reshape(queries.shape[0], -1, HD)
    scores = jnp.einsum("qhd,khd->hqk", queries, keys, preferred_element_type=jnp.float32)
    exponent = jnp.exp(scores)
    attention = (exponent / jnp.sum(exponent, axis=-1, keepdims=True)).astype(jnp.bfloat16)
    attended = jnp.einsum(
        "hqk,khd->qhd", attention, values, preferred_element_type=jnp.float32
    ).astype(jnp.bfloat16)
    attended = attended.reshape(attended.shape[0], -1)
    mixed = lax.psum_scatter(
        jnp.dot(attended, w_out[0], preferred_element_type=jnp.float32).astype(jnp.bfloat16),
        "tensor",
        scatter_dimension=0,
        tiled=True,
    )
    return mixed[None, None]


def solution(mesh):
    return jax.shard_map(
        body,
        mesh=mesh,
        in_specs=(
            P("dp", "section", None),
            P("section", "dp", "tensor", None),
            P(),
            P("section", None),
            P("section", None, "tensor"),
            P("section", None, "tensor"),
            P("section", None, "tensor"),
            P("section", "tensor", None),
        ),
        out_specs=P("section", "dp", "tensor", None),
        check_vma=False,
    )
```

profile of v0, /device:TPU:1, one launch (start us, length us, event | category | flops | bytes accessed | tf_op | source)
XLA Modules:
  0.0 280.6 jit_solution(6196544268101478378)
XLA Ops:
  6.5 0.0 copy-start
  6.5 0.0 all-gather.3.cloned.1.call-start
  6.5 0.0 copy-start.1
  6.5 2.4 multiply_reduce_fusion
  8.9 0.2 copy-done.1
  9.1 0.0 copy-start.4
  9.1 0.0 copy-start.3
  9.1 0.0 copy-start.2
  9.1 2.7 bitcast_convert_fusion
  11.8 0.0 copy-done.4
  11.8 0.1 dynamic-slice
  11.8 1.8 fusion.22
  13.6 0.0 all-gather.3.cloned.1.call-update
  13.7 0.0 all-gather.5.cloned.1.call-start
  13.7 0.0 copy-done.3
  13.7 0.0 copy-done.2
  13.8 0.1 fusion.23
  13.9 0.8 fusion.25
  14.7 0.0 all-gather.5.cloned.1.call-update
  14.7 0.0 reduce-scatter.2.cloned.1.call-start
  14.7 112.7 %all-gather.3.cloned.1.call-done = bf16[1152,4096]{1,0:T(8,128)(2,1)} async-done(((bf16[24,4096]{1,0:T(8,128)(2,1)}), bf16[1152,4096]{1,0:T(8,128)(2,1)}) %all-gather.3.cloned.1.call-update) | async-done | bytes 9437200 | tf_op jit(solution)/shard_map/all_gather | solution.py:25
  127.4 9.7 %fusion.4 = bf16[1152,512]{1,0:T(8,128)(2,1)} fusion(bf16[1152,4096]{1,0:T(8,128)(2,1)} %all-gather.3.cloned.1.call-done, bf16[4096,256]{1,0:T(8,128)(2,1)} %bitcast.36, bf16[4096,256]{1,0:T(8,128)(2,1)} %bitcast.37), kind=kOutput, calls=%fused_computation.6 | convolution fusion | flops 4840816640 | bytes 14811136 | tf_op jit(solution)/shard_map/dot_general | solution.py:24
  137.1 59.2 %all-gather.5.cloned.1.call-done = bf16[192,4096]{1,0:T(8,128)(2,1)} async-done(((bf16[16,4096]{1,0:T(8,128)(2,1)}), bf16[192,4096]{1,0:T(8,128)(2,1)}) %all-gather.5.cloned.1.call-update) | async-done | bytes 1572880 | tf_op jit(solution)/shard_map/all_gather | solution.py:32
  196.3 3.4 %fusion.27 = (f32[192]{0:T(256)S(1)}, f32[192,1152]{1,0:T(8,128)S(1)}) fusion(bf16[1152,512]{1,0:T(8,128)(2,1)} %fusion.4, bf16[192,4096]{1,0:T(8,128)(2,1)} %all-gather.5.cloned.1.call-done, bf16[1,4096,256]{2,1,0:T(8,128)(2,1)} %param.12), kind=kOutput, calls=%fused_computation.30 | convolution fusion | flops 516169536 | bytes 5145344 | tf_op jit(solution)/shard_map/qhd,khd->hqk/dot_general | solution.py:37
  199.6 0.0 copy-done
  199.6 3.3 %convolution_convert_fusion = bf16[192,4096]{1,0:T(8,128)(2,1)} fusion(bf16[1,256,4096]{2,1,0:T(8,128)(2,1)S(1)} %copy-done, bf16[1152,512]{1,0:T(8,128)(2,1)} %fusion.4, f32[192,1152]{1,0:T(8,128)S(1)} %get-tuple-element.6, f32[192]{0:T(256)S(1)} %get-tuple-element.5), kind=kOutput, calls=%fused_computation | convolution fusion | flops 517177344 | bytes 5145344 | tf_op jit(solution)/shard_map/dot_general | solution.py:45
  203.0 0.0 reduce-scatter.2.cloned.1.call-update
  203.0 71.1 %reduce-scatter.2.cloned.1.call-done = bf16[16,4096]{1,0:T(8,128)(2,1)} async-done(((bf16[192,4096]{1,0:T(8,128)(2,1)}), bf16[16,4096]{1,0:T(8,128)(2,1)}) %reduce-scatter.2.cloned.1.call-update) | async-done | bytes 131088 | tf_op jit(solution)/shard_map/reduce_scatter | solution.py:44
  (4 shorter events, 0.0 us)
Async XLA Ops:
  6.5 193.1 %copy-start = (bf16[1,256,4096]{2,1,0:T(8,128)(2,1)S(1)}, bf16[1,256,4096]{2,1,0:T(8,128)(2,1)}, u32[]{:S(2)}) copy-start(bf16[1,256,4096]{2,1,0:T(8,128)(2,1)} %param.15) | copy-start | bytes 6291460
  6.5 120.9 %all-gather.3.cloned.1.call-start = ((), (), s32[]{:S(2)}) async-start(), calls=%async_computation.1 | async-start | bytes 9633792 | tf_op jit(solution)/shard_map/all_gather | solution.py:25
  6.5 2.5 copy-start.1
  9.1 2.7 copy-start.4
  9.1 4.6 %copy-start.3 = (bf16[1,4096]{1,0:T(2,128)(2,1)S(1)}, bf16[1,4096]{1,0:T(2,128)(2,1)}, u32[]{:S(2)}) copy-start(bf16[1,4096]{1,0:T(2,128)(2,1)} %param.11) | copy-start | bytes 24580
  9.1 4.7 %copy-start.2 = (bf16[1,1,16,4096]{3,2,1,0:T(8,128)(2,1)S(1)}, bf16[1,1,16,4096]{3,2,1,0:T(8,128)(2,1)}, u32[]{:S(2)}) copy-start(bf16[1,1,16,4096]{3,2,1,0:T(8,128)(2,1)} %param.9) | copy-start | bytes 393220
  13.7 182.6 %all-gather.5.cloned.1.call-start = ((), (), s32[]{:S(2)}) async-start(), calls=%async_computation.2 | async-start | bytes 1703936 | tf_op jit(solution)/shard_map/all_gather | solution.py:32
  14.7 259.4 %reduce-scatter.2.cloned.1.call-start = ((), (), s32[]{:S(2)}) async-start(), calls=%async_computation.3 | async-start | bytes 1703936 | tf_op jit(solution)/shard_map/reduce_scatter | solution.py:44
Sparse Core Ops, SparseCore 0:
  13.8 113.5 all-gather.2
  129.8 66.4 all-gather.4
  203.1 70.9 reduce-scatter.1
where the time goes:
time: 285 us; the launch traced here: 281 us
  waiting for transfers between devices  243 us (85%)
  matrix products  16.4 us (6%)
  between operations  13.2 us (5%)
  other arithmetic  7.77 us (3%)
    all_gather x1, waiting for transfers between devices, body(): lax.all_gather(own_share, ('section', 'tensor'), axis=0, tiled=True)  113 us
    reduce_scatter x1, waiting for transfers between devices, body(): lax.psum_scatter(jnp.dot(attended, w_out[0], preferred_element_type=jnp.f...  71.1 us
    all_gather x1, waiting for transfers between devices, body(): lax.all_gather(normed, 'tensor', axis=0, tiled=True)  59.2 us
    dot_general x1, matrix products, body(): jnp.dot(lax.all_gather(own_share, ('section', 'tensor'), axis=0, tiled=Tr...  9.67 us
  transfers between devices with their start and end apart: 3, of which 3 were waited for; matrix products, arithmetic and copies ran while one was open for 4% of the time, Pallas kernels for 0%

commit v1 on v0

v1 whole, which is shorter than its diff:
```python
import functools

import jax
import jax.numpy as jnp
from jax import lax
from jax.experimental import pallas as pl
from jax.experimental.pallas import tpu as pltpu
from jax.sharding import PartitionSpec as P

F32 = jnp.float32
BF16 = jnp.bfloat16
MESH = pl.DeviceIdType.MESH

EX = 32
B1 = 16
B2 = 32
SHARED = B1 + 2 * B2
SPLIT = 2


def kernel(
    chips,
    enc_ref,
    dec_ref,
    enc_gain_ref,
    dec_gain_ref,
    wq_ref,
    wk_ref,
    wv_ref,
    wo_ref,
    out_ref,
    mem,
    dec,
    wq,
    wkv,
    wo,
    rms,
    dec_rms,
    kv,
    expo,
    part,
    to_core,
    from_core,
    to_line,
    from_line,
    send_sems,
    local_sems,
    x_sems,
    z_sems,
    core_sems,
    dec_sems,
    dec_core_sems,
    pair_sems,
    line_sems,
    line_send_sems,
):
    sections = lax.axis_size("section")
    s = lax.axis_index("section")
    t = lax.axis_index("tensor")
    z = t // 2
    c = t % 2
    e = z % 2
    last = chips - 1
    width = mem.shape[2]
    section_up = {"section": lax.rem(s + 1, sections)}
    section_down = {"section": lax.rem(s + sections - 1, sections)}
    other_core = {"tensor": t + 1 - 2 * c}
    z_partner = {"tensor": t + 2 - 4 * e}
    z_up = {"tensor": t + 2}
    z_down = {"tensor": t - 2}

    barrier = pltpu.get_barrier_semaphore()
    for target in (section_up, section_down, other_core):
        pl.semaphore_signal(barrier, inc=1, device_id=target, device_id_type=MESH)

    @pl.when(z < last)
    def _():
        pl.semaphore_signal(barrier, inc=1, device_id=z_up, device_id_type=MESH)

    @pl.when(z > 0)
    def _():
        pl.semaphore_signal(barrier, inc=1, device_id=z_down, device_id_type=MESH)

    locals_ = [
        pltpu.make_async_copy(src, dst, local_sems.at[i])
        for i, (src, dst) in enumerate(
            (
                (wk_ref.at[0], wkv.at[0]),
                (wv_ref.at[0], wkv.at[1]),
                (wq_ref.at[0], wq),
                (enc_ref.at[0], mem.at[0]),
                (dec_ref.at[0, 0], dec.at[t]),
                (wo_ref.at[0], wo),
            )
        )
    ]
    for copy in locals_:
        copy.start()

    pl.semaphore_wait(barrier, 3 + (z < last).astype(jnp.int32) + (z > 0).astype(jnp.int32))

    pending = []

    def send(src, dst, recv_sem, target, when=None):
        copy = pltpu.make_async_remote_copy(
            src_ref=src,
            dst_ref=dst,
            send_sem=send_sems.at[len(pending)],
            recv_sem=recv_sem,
            device_id=target,
            device_id_type=MESH,
        )
        pending.append((copy, when))
        if when is None:
            copy.start()
        else:
            pl.when(when)(copy.start)

    def arrived(dst, recv_sem):
        pltpu.make_async_remote_copy(
            src_ref=dst,
            dst_ref=dst,
            send_sem=send_sems.at[0],
            recv_sem=recv_sem,
            device_id=other_core,
            device_id_type=MESH,
        ).wait_recv()

    def piece_rows(piece, parity, core):
        if piece == 0:
            start, size = (2 * parity + core) * EX, EX
        elif piece == 1:
            start, size = 4 * EX + core * SHARED, B1
        else:
            start, size = 4 * EX + core * SHARED + B1 + (piece - 2) * B2, B2
        return pl.ds(pl.multiple_of(start, 16), size)

    for up_piece, down_piece in ((0, 0), (2, 1), (3, 2), (1, 3)):
        send(
            enc_ref.at[0, piece_rows(up_piece, e, c)],
            mem.at[2, piece_rows(up_piece, e, c)],
            x_sems.at[2, up_piece],
            section_up,
        )
        send(
            enc_ref.at[0, piece_rows(down_piece, e, c)],
            mem.at[1, piece_rows(down_piece, e, c)],
            x_sems.at[1, down_piece],
            section_down,
        )
    send(dec_ref.at[0, 0], dec.at[t], dec_sems.at[0, 1], z_up, z < last)
    send(dec_ref.at[0, 0], dec.at[t], dec_sems.at[1, 1], z_down, z > 0)
    send(dec_ref.at[0, 0], dec.at[t], dec_core_sems.at[0, 0], other_core)

    def from_x(slot, piece):
        block = mem.at[slot, piece_rows(piece, e, c)]
        arrived(block, x_sems.at[slot, piece])
        if slot == 1 and piece in (0, 1):
            target = mem.at[3, piece_rows(piece, e, c)]
            send(block, target, x_sems.at[3, piece], section_down)
        if slot == 2 and piece in (2, 3):
            target = mem.at[3, piece_rows(piece, e, c)]
            send(block, target, x_sems.at[3, piece], section_up)
        if piece == 0:
            send(block, block, z_sems.at[slot], z_partner)
        send(block, block, core_sems.at[slot, piece], other_core)

    def from_z(slot):
        block = mem.at[slot, piece_rows(0, 1 - e, c)]
        arrived(block, z_sems.at[slot])
        send(block, block, core_sems.at[slot, 4], other_core)

    def from_core_all(slot):
        for piece in range(4):
            arrived(mem.at[slot, piece_rows(piece, e, 1 - c)], core_sems.at[slot, piece])
        arrived(mem.at[slot, piece_rows(0, 1 - e, 1 - c)], core_sems.at[slot, 4])

    def from_decoder(k):
        below = z - k >= 0
        source = dec.at[jnp.maximum(t - 2 * k, 0)]

        @pl.when(below)
        def _():
            arrived(source, dec_sems.at[0, k])

        if k < last:
            send(source, source, dec_sems.at[0, k + 1], z_up, below & (z < last))
        send(source, source, dec_core_sems.at[0, k], other_core, below)
        above = z + k <= last
        source_ = dec.at[jnp.minimum(t + 2 * k, 2 * chips - 1)]

        @pl.when(above)
        def _():
            arrived(source_, dec_sems.at[1, k])

        if k < last:
            send(source_, source_, dec_sems.at[1, k + 1], z_down, above & (z > 0))
        send(source_, source_, dec_core_sems.at[1, k], other_core, above)

    def decoder_from_core():
        arrived(dec.at[t + 1 - 2 * c], dec_core_sems.at[0, 0])
        for k in range(1, chips):

            @pl.when(z - k >= 0)
            def _():
                source = dec.at[jnp.maximum(t - 2 * k + 1 - 2 * c, 0)]
                arrived(source, dec_core_sems.at[0, k])

            @pl.when(z + k <= last)
            def _():
                source = dec.at[jnp.minimum(t + 2 * k + 1 - 2 * c, 2 * chips - 1)]
                arrived(source, dec_core_sems.at[1, k])

    def project(slot):
        def row_group(i, carry):
            rows = pl.ds(pl.multiple_of(i * 16, 16), 16)
            x = mem[slot, rows, :].astype(F32)
            mean_sq = jnp.sum(x * x, axis=-1, keepdims=True) * (1.0 / width)
            rms[rows, :] = lax.rsqrt(mean_sq + 1e-06)
            return carry

        lax.fori_loop(0, mem.shape[1] // 16, row_group, 0)

        def side(n, carry):
            projected = jnp.dot(mem[slot], wkv[n], preferred_element_type=F32)
            kv[n, slot] = (projected * rms[...]).astype(BF16)
            return carry

        lax.fori_loop(0, 2, side, 0)

    locals_[0].wait()
    locals_[1].wait()
    locals_[2].wait()

    def fold(i, carry):
        start = pl.multiple_of(i * 128, 128)
        rows = pl.ds(start, 128)
        enc_gain = jnp.broadcast_to(enc_gain_ref[:, pl.ds(start, 128)].astype(F32), (128, 128)).T
        dec_gain = jnp.broadcast_to(dec_gain_ref[:, pl.ds(start, 128)].astype(F32), (128, 128)).T
        for half in range(wq.shape[1] // 128):
            columns = pl.ds(half * 128, 128)
            for n in range(2):
                wkv[n, rows, columns] = (wkv[n, rows, columns].astype(F32) * enc_gain).astype(BF16)
            wq[rows, columns] = (wq[rows, columns].astype(F32) * dec_gain).astype(BF16)
        return carry

    lax.fori_loop(0, width // 128, fold, 0)

    from_decoder(1)
    from_x(1, 0)
    from_x(2, 0)
    from_decoder(2)
    locals_[3].wait()
    project(0)
    from_decoder(3) if chips > 3 else None
    from_x(1, 1)
    from_x(2, 2)
    from_z(1)
    from_z(2)
    from_decoder(4) if chips > 4 else None
    from_x(1, 2)
    from_x(2, 3)
    from_decoder(5) if chips > 5 else None
    locals_[4].wait()
    decoder_from_core()

    def decoder_rows(i, carry):
        x = dec[i].astype(F32)
        mean_sq = jnp.sum(x * x, axis=-1, keepdims=True) * (1.0 / width)
        dec_rms[i] = lax.rsqrt(mean_sq + 1e-06)
        return carry

    lax.fori_loop(0, 2 * chips, decoder_rows, 0)
    tokens = 2 * chips * dec.shape[1]
    queries = jnp.dot(dec[...].reshape(tokens, width), wq[...], preferred_element_type=F32)
    queries = (queries * dec_rms[...].reshape(tokens, 1)).astype(BF16)

    def score(slot):
        scores = lax.dot_general(
            queries, kv[0, slot], (((1,), (1,)), ((), ())), preferred_element_type=F32
        )
        exponent = jnp.exp(scores)
        expo[slot] = exponent
        return jnp.sum(exponent, axis=-1, keepdims=True)

    total = score(0)
    from_x(1, 3)
    from_x(2, 1)
    from_core_all(1)
    project(1)
    from_x(3, 0)
    from_core_all(2)
    project(2)
    from_x(3, 1)
    from_x(3, 2)
    total += score(1)
    total += score(2)
    from_x(3, 3)
    from_z(3)
    from_core_all(3)
    project(3)
    total += score(3)
    inverse = 1.0 / total
    attended = jnp.zeros((tokens, kv.shape[3]), F32)
    for slot in range(4):
        attention = (expo[slot] * inverse).astype(BF16)
        attended += jnp.dot(attention, kv[1, slot], preferred_element_type=F32)
    attended = attended.astype(BF16)
    locals_[5].wait()

    tile = min(512, width)
    for n in range(width // tile):
        columns = pl.ds(n * tile, tile)
        product = jnp.dot(attended, wo[:, columns], preferred_element_type=F32)
        part[:, :, columns] = product.reshape(2 * chips, dec.shape[1], tile)

    first = (z >= chips // 2).astype(jnp.int32)

    def line(direction, k):
        position = jnp.where(direction == 0, z, last - z)
        dest = jnp.where(direction == 0, last - k, k)
        return position, dest

    pair = []
    for k in range(chips):
        _, dest = line(first, k)
        to_core[dest] = part[2 * dest + 1 - c].astype(BF16)
        copy = pltpu.make_async_remote_copy(
            src_ref=to_core.at[dest],
            dst_ref=from_core.at[dest],
            send_sem=pair_sems.at[0, k],
            recv_sem=pair_sems.at[1, k],
            device_id=other_core,
            device_id_type=MESH,
        )
        copy.start()
        pair.append(copy)

    piece_width = width // SPLIT
    sent = []

    def pass_on(direction, k):
        position, dest = line(direction, k)
        active = last - k > position
        for h in range(SPLIT):
            columns = pl.ds(h * piece_width, piece_width)
            landed = from_line.at[direction, dest, h]
            copy = pltpu.make_async_remote_copy(
                src_ref=to_line.at[direction, dest, h],
                dst_ref=landed,
                send_sem=line_send_sems.at[direction, k, h],
                recv_sem=line_sems.at[direction, k, h],
                device_id={"tensor": t + 2 - 4 * direction},
                device_id_type=MESH,
            )
            own = lambda: part[2 * dest + c, :, columns] + from_core[dest, :, columns].astype(F32)

            @pl.when(active & (position == 0))
            def _():
                to_line[direction, dest, h] = own().astype(BF16)
                copy.start()

            @pl.when(active & (position > 0))
            def _():
                arrived(landed, line_sems.at[direction, k, h])
                value = own() + from_line[direction, dest, h].astype(F32)
                to_line[direction, dest, h] = value.astype(BF16)
                copy.start()

            sent.append((copy, active))

    for k in range(chips):
        pair[k].wait_recv()
        if k < last:
            pass_on(first, k)
    for k in range(last - (chips + 1) // 2):
        pass_on(1 - first, k)

    for h in range(SPLIT):
        columns = pl.ds(h * piece_width, piece_width)
        part[t, :, columns] += from_core[z, :, columns].astype(F32)

        @pl.when(z > 0)
        def _():
            arrived(from_line.at[0, z, h], line_sems.at[0, last - z, h])
            part[t, :, columns] += from_line[0, z, h].astype(F32)

        @pl.when(z < last)
        def _():
            arrived(from_line.at[1, z, h], line_sems.at[1, z, h])
            part[t, :, columns] += from_line[1, z, h].astype(F32)

        out_ref[:, columns] = part[t, :, columns].astype(BF16)

    for copy, when in pending + sent:
        if when is None:
            copy.wait_send()
        else:
            pl.when(when)(copy.wait_send)
    for copy in pair:
        copy.wait_send()


def body(enc_hidden, dec_hidden, enc_gain, dec_gain, w_query, w_key, w_value, w_out):
    chips = lax.axis_size("tensor") // 2
    rows, width = enc_hidden.shape[1:]
    share = dec_hidden.shape[2]
    head = w_query.shape[2]
    any_space = pl.BlockSpec(memory_space=pl.ANY)
    vmem = pl.BlockSpec(memory_space=pltpu.VMEM)
    dma = pltpu.SemaphoreType.DMA
    mixed = pl.pallas_call(
        functools.partial(kernel, chips),
        out_shape=jax.ShapeDtypeStruct((share, width), BF16),
        in_specs=[any_space, any_space, vmem, vmem] + [any_space] * 4,
        out_specs=vmem,
        scratch_shapes=[
            pltpu.VMEM((4, rows, width), BF16),
            pltpu.VMEM((2 * chips, share, width), BF16),
            pltpu.VMEM((width, head), BF16),
            pltpu.VMEM((2, width, head), BF16),
            pltpu.VMEM((head, width), BF16),
            pltpu.VMEM((rows, 1), F32),
            pltpu.VMEM((2 * chips, share, 1), F32),
            pltpu.VMEM((2, 4, rows, head), BF16),
            pltpu.VMEM((4, 2 * chips * share, rows), F32),
            pltpu.VMEM((2 * chips, share, width), F32),
            pltpu.VMEM((chips, share, width), BF16),
            pltpu.VMEM((chips, share, width), BF16),
            pltpu.VMEM((2, chips, SPLIT, share, width // SPLIT), BF16),
            pltpu.VMEM((2, chips, SPLIT, share, width // SPLIT), BF16),
            dma((64,)),
            dma((6,)),
            dma((4, 4)),
            dma((4,)),
            dma((4, 5)),
            dma((2, chips + 1)),
            dma((2, chips)),
            dma((2, chips)),
            dma((2, chips, SPLIT)),
            dma((2, chips, SPLIT)),
        ],
        compiler_params=pltpu.CompilerParams(
            collective_id=0, has_side_effects=True, vmem_limit_bytes=60 * 1024 * 1024
        ),
        name="cross_attention",
    )(
        enc_hidden,
        dec_hidden,
        enc_gain.reshape(1, width),
        dec_gain,
        w_query,
        w_key,
        w_value,
        w_out,
    )
    return mixed[None, None]


def solution(mesh):
    return jax.shard_map(
        body,
        mesh=mesh,
        in_specs=(
            P("dp", "section", None),
            P("section", "dp", "tensor", None),
            P(),
            P("section", None),
            P("section", None, "tensor"),
            P("section", None, "tensor"),
            P("section", None, "tensor"),
            P("section", "tensor", None),
        ),
        out_specs=P("section", "dp", "tensor", None),
        check_vma=False,
    )
```

time: 285 us -> 89.5 us (0.31)
  the two profiles are of different devices: /device:TPU:1 before, /device:TPU:32 now
where the time goes in v1:
time: 89.5 us; the launch traced here: 89.2 us
  Pallas kernels  86.3 us (96%)
  local copies, waits for them, and re-layouts  2.88 us (3%)
    pallas_call x1, Pallas kernels, body(): pl.pallas_call(functools.partial(kernel, chips), out_shape=jax.ShapeDtype...  86.3 us

profile of v1, /device:TPU:32, one launch (start us, length us, event | category | flops | bytes accessed | tf_op | source)
XLA Modules:
  0.0 89.2 jit_solution(9028137279367322015)
XLA Ops:
  0.0 1.3 %reshape.3.enc_gain_ref = bf16[1,4096]{1,0:T(2,128)(2,1)} reshape(bf16[4096]{0:T(1024)(128)(2,1)} %param.10) | data formatting | bytes 16384 | tf_op jit(solution)/shard_map/reshape | solution.py:450
  1.3 86.3 %cross_attention.1 = bf16[16,4096]{1,0:T(8,128)(2,1)} custom-call(bf16[1,288,4096]{2,1,0:T(8,128)(2,1)} %enc_ref.1, bf16[1,1,16,4096]{3,2,1,0:T(8,128)(2,1)} %dec_ref.1, bf16[1,4096]{1,0:T(2,128)(2,1)} %reshape.3.enc_gain_ref, bf16[1,4096]{1,0:T(2,128)(2,1)} %dec_gain_ref.1, bf16[1,4096,256]{2,1,0:T(8,128)(2,1)} %wq_ref.1, bf16[1,4096,256]{2,1,0:T(8,128)(2,1)} %wk_ref.1, ...), custom_call_target="tpu_custom_call" | custom-call | tf_op jit(solution)/shard_map/cross_attention/pallas_call | solution.py:412
  87.6 1.6 %copy.10 = bf16[1,1,16,4096]{3,2,1,0:T(8,128)(2,1)} copy(bf16[1,1,16,4096]{3,2,1,0:T(8,128)(2,1)} %bitcast.1) | data formatting | bytes 262144

commit v2 on v1

--- a/solution.py
+++ b/solution.py
@@ -34,13 +34,14 @@
     wq,
     wkv,
     wo,
-    rms,
-    dec_rms,
+    gain,
+    query,
+    total,
     kv,
     expo,
     part,
     to_core,
-    from_core,
+    from_core_rows,
     to_line,
     from_line,
     send_sems,
@@ -81,21 +82,40 @@
     def _():
         pl.semaphore_signal(barrier, inc=1, device_id=z_down, device_id_type=MESH)
 
-    locals_ = [
-        pltpu.make_async_copy(src, dst, local_sems.at[i])
-        for i, (src, dst) in enumerate(
-            (
-                (wk_ref.at[0], wkv.at[0]),
-                (wv_ref.at[0], wkv.at[1]),
-                (wq_ref.at[0], wq),
-                (enc_ref.at[0], mem.at[0]),
-                (dec_ref.at[0, 0], dec.at[t]),
-                (wo_ref.at[0], wo),
-            )
-        )
-    ]
-    for copy in locals_:
+    def exchange_rows(index):
+        return pl.ds(pl.multiple_of(index * EX, 16), EX)
+
+    def shared_rows(core):
+        return pl.ds(pl.multiple_of(4 * EX + core * SHARED, 16), SHARED)
+
+    own = 2 * e + c
+    others = [lax.rem(own + i, 4) for i in (1, 2, 3)]
+    enc = [exchange_rows(own), shared_rows(c)] + [exchange_rows(i) for i in others] + [shared_rows(1 - c)]
+    moves = [(enc_ref.at[0, rows], mem.at[0, rows]) for rows in enc]
+    moves.insert(1, (dec_ref.at[0, 0], dec.at[t]))
+    moves += [(wk_ref.at[0], wkv.at[0]), (wv_ref.at[0], wkv.at[1]), (wq_ref.at[0], wq), (wo_ref.at[0], wo)]
+    loads = [pltpu.make_async_copy(src, dst, local_sems.at[i]) for i, (src, dst) in enumerate(moves)]
+    for copy in loads:
         copy.start()
+
+    def normalize(hidden, factor):
+        values = hidden.astype(F32)
+        mean_sq = jnp.sum(values * values, axis=-1, keepdims=True) * (1.0 / width)
+        return (values * lax.rsqrt(mean_sq + 1e-06) * factor).astype(BF16)
+
+    def normalize_rows(start, size):
+        def group(i, carry):
+            rows = pl.ds(pl.multiple_of(start + i * 16, 16), 16)
+            mem[0, rows, :] = normalize(mem[0, rows, :], gain[...])
+            return carry
+
+        lax.fori_loop(0, size // 16, group, 0)
+
+    gain[...] = enc_gain_ref[...].reshape(1, width).astype(F32)
+    loads[0].wait()
+    normalize_rows(own * EX, EX)
+    loads[1].wait()
+    dec[t] = normalize(dec[t], dec_gain_ref[...].astype(F32))
 
     pl.semaphore_wait(barrier, 3 + (z < last).astype(jnp.int32) + (z > 0).astype(jnp.int32))
 
@@ -135,22 +155,27 @@
             start, size = 4 * EX + core * SHARED + B1 + (piece - 2) * B2, B2
         return pl.ds(pl.multiple_of(start, 16), size)
 
-    for up_piece, down_piece in ((0, 0), (2, 1), (3, 2), (1, 3)):
+    def to_x(slot, piece):
+        rows = piece_rows(piece, e, c)
         send(
-            enc_ref.at[0, piece_rows(up_piece, e, c)],
-            mem.at[2, piece_rows(up_piece, e, c)],
-            x_sems.at[2, up_piece],
-            section_up,
+            mem.at[0, rows],
+            mem.at[slot, rows],
+            x_sems.at[slot, piece],
+            section_up if slot == 2 else section_down,
         )
-        send(
-            enc_ref.at[0, piece_rows(down_piece, e, c)],
-            mem.at[1, piece_rows(down_piece, e, c)],
-            x_sems.at[1, down_piece],
-            section_down,
-        )
-    send(dec_ref.at[0, 0], dec.at[t], dec_sems.at[0, 1], z_up, z < last)
-    send(dec_ref.at[0, 0], dec.at[t], dec_sems.at[1, 1], z_down, z > 0)
-    send(dec_ref.at[0, 0], dec.at[t], dec_core_sems.at[0, 0], other_core)
+
+    to_x(2, 0)
+    to_x(1, 0)
+    send(dec.at[t], dec.at[t], dec_sems.at[0, 1], z_up, z < last)
+    send(dec.at[t], dec.at[t], dec_sems.at[1, 1], z_down, z > 0)
+    send(dec.at[t], dec.at[t], dec_core_sems.at[0, 0], other_core)
+    loads[2].wait()
+    normalize_rows(4 * EX + c * SHARED, SHARED)
+    to_x(2, 2)
+    to_x(1, 1)
+    to_x(1, 2)
+    to_x(2, 3)
+    to_x(2, 1)
 
     def from_x(slot, piece):
         block = mem.at[slot, piece_rows(piece, e, c)]
@@ -170,10 +195,10 @@
         arrived(block, z_sems.at[slot])
         send(block, block, core_sems.at[slot, 4], other_core)
 
-    def from_core_all(slot):
-        for piece in range(4):
-            arrived(mem.at[slot, piece_rows(piece, e, 1 - c)], core_sems.at[slot, piece])
-        arrived(mem.at[slot, piece_rows(0, 1 - e, 1 - c)], core_sems.at[slot, 4])
+    def from_core(slot, pieces):
+        for piece in pieces:
+            parity = 1 - e if piece == 4 else e
+            arrived(mem.at[slot, piece_rows(piece % 4, parity, 1 - c)], core_sems.at[slot, piece])
 
     def from_decoder(k):
         below = z - k >= 0
@@ -211,108 +236,96 @@
                 source = dec.at[jnp.minimum(t + 2 * k + 1 - 2 * c, 2 * chips - 1)]
                 arrived(source, dec_core_sems.at[1, k])
 
-    def project(slot):
-        def row_group(i, carry):
-            rows = pl.ds(pl.multiple_of(i * 16, 16), 16)
-            x = mem[slot, rows, :].astype(F32)
-            mean_sq = jnp.sum(x * x, axis=-1, keepdims=True) * (1.0 / width)
-            rms[rows, :] = lax.rsqrt(mean_sq + 1e-06)
+    def project(slot, start, size):
+        def side(n, carry):
+            block = mem[slot, start : start + size, :]
+            projected = jnp.dot(block, wkv[n], preferred_element_type=F32)
+            kv[n, slot, start : start + size, :] = projected.astype(BF16)
             return carry
 
-        lax.fori_loop(0, mem.shape[1] // 16, row_group, 0)
-
-        def side(n, carry):
-            projected = jnp.dot(mem[slot], wkv[n], preferred_element_type=F32)
-            kv[n, slot] = (projected * rms[...]).astype(BF16)
-            return carry
-
         lax.fori_loop(0, 2, side, 0)
 
-    locals_[0].wait()
-    locals_[1].wait()
-    locals_[2].wait()
-
-    def fold(i, carry):
-        start = pl.multiple_of(i * 128, 128)
-        rows = pl.ds(start, 128)
-        enc_gain = jnp.broadcast_to(enc_gain_ref[:, pl.ds(start, 128)].astype(F32), (128, 128)).T
-        dec_gain = jnp.broadcast_to(dec_gain_ref[:, pl.ds(start, 128)].astype(F32), (128, 128)).T
-        for half in range(wq.shape[1] // 128):
-            columns = pl.ds(half * 128, 128)
-            for n in range(2):
-                wkv[n, rows, columns] = (wkv[n, rows, columns].astype(F32) * enc_gain).astype(BF16)
-            wq[rows, columns] = (wq[rows, columns].astype(F32) * dec_gain).astype(BF16)
-        return carry
-
-    lax.fori_loop(0, width // 128, fold, 0)
-
+    blocks = mem.shape[1]
+    tokens = 2 * chips * dec.shape[1]
+
+    def scores_of(slot, rows):
+        scores = lax.dot_general(
+            query[rows, :], kv[0, slot], (((1,), (1,)), ((), ())), preferred_element_type=F32
+        )
+        exponent = jnp.exp(scores)
+        return exponent, jnp.sum(exponent, axis=-1, keepdims=True)
+
+    def score(slot):
+        exponent, row_sum = scores_of(slot, pl.ds(0, tokens))
+        expo[slot] = exponent
+        return row_sum
+
+    for i, index in enumerate(others):
+        loads[3 + i].wait()
+        normalize_rows(index * EX, EX)
+    loads[6].wait()
+    normalize_rows(4 * EX + (1 - c) * SHARED, SHARED)
     from_decoder(1)
     from_x(1, 0)
+    to_x(1, 3)
     from_x(2, 0)
-    from_decoder(2)
-    locals_[3].wait()
-    project(0)
-    from_decoder(3) if chips > 3 else None
+    if chips > 2:
+        from_decoder(2)
+    loads[7].wait()
+    loads[8].wait()
+    project(0, 0, blocks)
     from_x(1, 1)
+    if chips > 3:
+        from_decoder(3)
     from_x(2, 2)
+    from_x(1, 2)
+    if chips > 4:
+        from_decoder(4)
+    from_x(2, 3)
+    from_x(2, 1)
+    from_x(3, 0)
     from_z(1)
     from_z(2)
-    from_decoder(4) if chips > 4 else None
-    from_x(1, 2)
-    from_x(2, 3)
-    from_decoder(5) if chips > 5 else None
-    locals_[4].wait()
+    if chips > 5:
+        from_decoder(5)
     decoder_from_core()
-
-    def decoder_rows(i, carry):
-        x = dec[i].astype(F32)
-        mean_sq = jnp.sum(x * x, axis=-1, keepdims=True) * (1.0 / width)
-        dec_rms[i] = lax.rsqrt(mean_sq + 1e-06)
-        return carry
-
-    lax.fori_loop(0, 2 * chips, decoder_rows, 0)
-    tokens = 2 * chips * dec.shape[1]
+    loads[9].wait()
     queries = jnp.dot(dec[...].reshape(tokens, width), wq[...], preferred_element_type=F32)
-    queries = (queries * dec_rms[...].reshape(tokens, 1)).astype(BF16)
-
-    def score(slot):
-        scores = lax.dot_general(
-            queries, kv[0, slot], (((1,), (1,)), ((), ())), preferred_element_type=F32
-        )
-        exponent = jnp.exp(scores)
-        expo[slot] = exponent
-        return jnp.sum(exponent, axis=-1, keepdims=True)
-
-    total = score(0)
+    query[...] = queries.astype(BF16)
+    total[...] = score(0)
+    from_core(2, range(5))
+    project(2, 0, blocks)
     from_x(1, 3)
-    from_x(2, 1)
-    from_core_all(1)
-    project(1)
-    from_x(3, 0)
-    from_core_all(2)
-    project(2)
+    from_x(3, 2)
+    from_z(3)
+    total[...] += score(2)
+    from_core(1, range(5))
+    project(1, 0, blocks)
     from_x(3, 1)
-    from_x(3, 2)
-    total += score(1)
-    total += score(2)
+    total[...] += score(1)
+    from_core(3, (0, 4))
+    project(3, 0, 4 * EX)
     from_x(3, 3)
-    from_z(3)
-    from_core_all(3)
-    project(3)
-    total += score(3)
-    inverse = 1.0 / total
-    attended = jnp.zeros((tokens, kv.shape[3]), F32)
-    for slot in range(4):
-        attention = (expo[slot] * inverse).astype(BF16)
-        attended += jnp.dot(attention, kv[1, slot], preferred_element_type=F32)
-    attended = attended.astype(BF16)
-    locals_[5].wait()
-
-    tile = min(512, width)
-    for n in range(width // tile):
-        columns = pl.ds(n * tile, tile)
-        product = jnp.dot(attended, wo[:, columns], preferred_element_type=F32)
-        part[:, :, columns] = product.reshape(2 * chips, dec.shape[1], tile)
+    from_core(3, (1, 2, 3))
+    project(3, 4 * EX, blocks - 4 * EX)
+    loads[10].wait()
+
+    def attend(start, size):
+        rows = pl.ds(pl.multiple_of(start, 16), size)
+        exponent, row_sum = scores_of(3, rows)
+        inverse = 1.0 / (total[rows, :] + row_sum)
+        attention = (exponent * inverse).astype(BF16)
+        attended = jnp.dot(attention, kv[1, 3], preferred_element_type=F32)
+        for slot in range(3):
+            attention = (expo[slot, rows, :] * inverse).astype(BF16)
+            attended += jnp.dot(attention, kv[1, slot], preferred_element_type=F32)
+        attended = attended.astype(BF16)
+        tile = min(512, width)
+        share = dec.shape[1]
+        for n in range(width // tile):
+            columns = pl.ds(n * tile, tile)
+            product = jnp.dot(attended, wo[:, columns], preferred_element_type=F32)
+            part[pl.ds(start // share, size // share), :, columns] = product.reshape(size // share, share, tile)
 
     first = (z >= chips // 2).astype(jnp.int32)
 
@@ -322,12 +335,13 @@
         return position, dest
 
     pair = []
-    for k in range(chips):
+
+    def swap(k):
         _, dest = line(first, k)
         to_core[dest] = part[2 * dest + 1 - c].astype(BF16)
         copy = pltpu.make_async_remote_copy(
             src_ref=to_core.at[dest],
-            dst_ref=from_core.at[dest],
+            dst_ref=from_core_rows.at[dest],
             send_sem=pair_sems.at[0, k],
             recv_sem=pair_sems.at[1, k],
             device_id=other_core,
@@ -353,23 +367,33 @@
                 device_id={"tensor": t + 2 - 4 * direction},
                 device_id_type=MESH,
             )
-            own = lambda: part[2 * dest + c, :, columns] + from_core[dest, :, columns].astype(F32)
+            mine = lambda: part[2 * dest + c, :, columns] + from_core_rows[dest, :, columns].astype(F32)
 
             @pl.when(active & (position == 0))
             def _():
-                to_line[direction, dest, h] = own().astype(BF16)
+                to_line[direction, dest, h] = mine().astype(BF16)
                 copy.start()
 
             @pl.when(active & (position > 0))
             def _():
                 arrived(landed, line_sems.at[direction, k, h])
-                value = own() + from_line[direction, dest, h].astype(F32)
+                value = mine() + from_line[direction, dest, h].astype(F32)
                 to_line[direction, dest, h] = value.astype(BF16)
                 copy.start()
 
             sent.append((copy, active))
 
-    for k in range(chips):
+    half = tokens // 2
+    far = half * (1 - first)
+    attend(far, half)
+    for k in range(chips // 2):
+        swap(k)
+    pair[0].wait_recv()
+    pass_on(first, 0)
+    attend(half - far, half)
+    for k in range(chips // 2, chips):
+        swap(k)
+    for k in range(1, chips):
         pair[k].wait_recv()
         if k < last:
             pass_on(first, k)
@@ -378,7 +402,7 @@
 
     for h in range(SPLIT):
         columns = pl.ds(h * piece_width, piece_width)
-        part[t, :, columns] += from_core[z, :, columns].astype(F32)
+        part[t, :, columns] += from_core_rows[z, :, columns].astype(F32)
 
         @pl.when(z > 0)
         def _():
@@ -420,8 +444,9 @@
             pltpu.VMEM((width, head), BF16),
             pltpu.VMEM((2, width, head), BF16),
             pltpu.VMEM((head, width), BF16),
-            pltpu.VMEM((rows, 1), F32),
-            pltpu.VMEM((2 * chips, share, 1), F32),
+            pltpu.VMEM((1, width), F32),
+            pltpu.VMEM((2 * chips * share, head), BF16),
+            pltpu.VMEM((2 * chips * share, 1), F32),
             pltpu.VMEM((2, 4, rows, head), BF16),
             pltpu.VMEM((4, 2 * chips * share, rows), F32),
             pltpu.VMEM((2 * chips, share, width), F32),
@@ -430,7 +455,7 @@
             pltpu.VMEM((2, chips, SPLIT, share, width // SPLIT), BF16),
             pltpu.VMEM((2, chips, SPLIT, share, width // SPLIT), BF16),
             dma((64,)),
-            dma((6,)),
+            dma((11,)),
             dma((4, 4)),
             dma((4,)),
             dma((4, 5)),
@@ -447,7 +472,7 @@
     )(
         enc_hidden,
         dec_hidden,
-        enc_gain.reshape(1, width),
+        enc_gain,
         dec_gain,
         w_query,
         w_key,

time: 89.5 us -> 80.6 us (0.901)
  the two profiles are of different devices: /device:TPU:32 before, /device:TPU:40 now
where the time goes in v2:
time: 80.6 us; the launch traced here: 80.4 us
  Pallas kernels  78.8 us (98%)
  local copies, waits for them, and re-layouts  1.57 us (2%)
    pallas_call x1, Pallas kernels, body(): pl.pallas_call(functools.partial(kernel, chips), out_shape=jax.ShapeDtype...  78.8 us

profile of v2, /device:TPU:40, one launch (start us, length us, event | category | flops | bytes accessed | tf_op | source)
XLA Modules:
  0.0 80.4 jit_solution(808290005815305864)
XLA Ops:
  0.0 78.8 %cross_attention.1 = bf16[16,4096]{1,0:T(8,128)(2,1)} custom-call(bf16[1,288,4096]{2,1,0:T(8,128)(2,1)} %enc_ref.1, bf16[1,1,16,4096]{3,2,1,0:T(8,128)(2,1)} %dec_ref.1, bf16[4096]{0:T(1024)(128)(2,1)} %enc_gain_ref.1, bf16[1,4096]{1,0:T(2,128)(2,1)} %dec_gain_ref.1, bf16[1,4096,256]{2,1,0:T(8,128)(2,1)} %wq_ref.1, bf16[1,4096,256]{2,1,0:T(8,128)(2,1)} %wk_ref.1, ...), custom_call_target="tpu_custom_call" | custom-call | tf_op jit(solution)/shard_map/cross_attention/pallas_call | solution.py:436
  78.8 1.6 %copy.10 = bf16[1,1,16,4096]{3,2,1,0:T(8,128)(2,1)} copy(bf16[1,1,16,4096]{3,2,1,0:T(8,128)(2,1)} %bitcast.1) | data formatting | bytes 262144

commit v3 on v2

--- a/solution.py
+++ b/solution.py
@@ -15,7 +15,7 @@
 B1 = 16
 B2 = 32
 SHARED = B1 + 2 * B2
-SPLIT = 2
+SPLIT = 4
 
 
 def kernel(
@@ -82,15 +82,23 @@
     def _():
         pl.semaphore_signal(barrier, inc=1, device_id=z_down, device_id_type=MESH)
 
+    def piece_rows(piece, parity, core):
+        if piece == 0:
+            start, size = (2 * parity + core) * EX, EX
+        elif piece == 2:
+            start, size = 4 * EX + core * B2, B2
+        elif piece == 1:
+            start, size = 4 * EX + 2 * B2 + core * B1, B1
+        else:
+            start, size = 4 * EX + 2 * B2 + 2 * B1 + core * B2, B2
+        return pl.ds(pl.multiple_of(start, 16), size)
+
     def exchange_rows(index):
         return pl.ds(pl.multiple_of(index * EX, 16), EX)
 
-    def shared_rows(core):
-        return pl.ds(pl.multiple_of(4 * EX + core * SHARED, 16), SHARED)
-
     own = 2 * e + c
     others = [lax.rem(own + i, 4) for i in (1, 2, 3)]
-    enc = [exchange_rows(own), shared_rows(c)] + [exchange_rows(i) for i in others] + [shared_rows(1 - c)]
+    enc = [exchange_rows(own), pl.ds(4 * EX, 2 * SHARED)] + [exchange_rows(i) for i in others]
     moves = [(enc_ref.at[0, rows], mem.at[0, rows]) for rows in enc]
     moves.insert(1, (dec_ref.at[0, 0], dec.at[t]))
     moves += [(wk_ref.at[0], wkv.at[0]), (wv_ref.at[0], wkv.at[1]), (wq_ref.at[0], wq), (wo_ref.at[0], wo)]
@@ -103,7 +111,9 @@
         mean_sq = jnp.sum(values * values, axis=-1, keepdims=True) * (1.0 / width)
         return (values * lax.rsqrt(mean_sq + 1e-06) * factor).astype(BF16)
 
-    def normalize_rows(start, size):
+    def normalize_rows(rows):
+        start, size = rows.start, rows.size
+
         def group(i, carry):
             rows = pl.ds(pl.multiple_of(start + i * 16, 16), 16)
             mem[0, rows, :] = normalize(mem[0, rows, :], gain[...])
@@ -113,7 +123,7 @@
 
     gain[...] = enc_gain_ref[...].reshape(1, width).astype(F32)
     loads[0].wait()
-    normalize_rows(own * EX, EX)
+    normalize_rows(exchange_rows(own))
     loads[1].wait()
     dec[t] = normalize(dec[t], dec_gain_ref[...].astype(F32))
 
@@ -146,15 +156,6 @@
             device_id_type=MESH,
         ).wait_recv()
 
-    def piece_rows(piece, parity, core):
-        if piece == 0:
-            start, size = (2 * parity + core) * EX, EX
-        elif piece == 1:
-            start, size = 4 * EX + core * SHARED, B1
-        else:
-            start, size = 4 * EX + core * SHARED + B1 + (piece - 2) * B2, B2
-        return pl.ds(pl.multiple_of(start, 16), size)
-
     def to_x(slot, piece):
         rows = piece_rows(piece, e, c)
         send(
@@ -170,10 +171,11 @@
     send(dec.at[t], dec.at[t], dec_sems.at[1, 1], z_down, z > 0)
     send(dec.at[t], dec.at[t], dec_core_sems.at[0, 0], other_core)
     loads[2].wait()
-    normalize_rows(4 * EX + c * SHARED, SHARED)
+    normalize_rows(piece_rows(2, e, c))
     to_x(2, 2)
+    normalize_rows(piece_rows(1, e, c))
     to_x(1, 1)
-    to_x(1, 2)
+    normalize_rows(piece_rows(3, e, c))
     to_x(2, 3)
     to_x(2, 1)
 
@@ -262,53 +264,56 @@
 
     for i, index in enumerate(others):
         loads[3 + i].wait()
-        normalize_rows(index * EX, EX)
-    loads[6].wait()
-    normalize_rows(4 * EX + (1 - c) * SHARED, SHARED)
+        normalize_rows(exchange_rows(index))
     from_decoder(1)
     from_x(1, 0)
+    to_x(1, 2)
     to_x(1, 3)
     from_x(2, 0)
+    for piece in (1, 2, 3):
+        normalize_rows(piece_rows(piece, e, 1 - c))
     if chips > 2:
         from_decoder(2)
+    loads[6].wait()
     loads[7].wait()
-    loads[8].wait()
     project(0, 0, blocks)
     from_x(1, 1)
     if chips > 3:
         from_decoder(3)
     from_x(2, 2)
-    from_x(1, 2)
+    from_x(3, 0)
     if chips > 4:
         from_decoder(4)
     from_x(2, 3)
+    from_z(1)
     from_x(2, 1)
-    from_x(3, 0)
-    from_z(1)
     from_z(2)
     if chips > 5:
         from_decoder(5)
     decoder_from_core()
-    loads[9].wait()
+    loads[8].wait()
     queries = jnp.dot(dec[...].reshape(tokens, width), wq[...], preferred_element_type=F32)
     query[...] = queries.astype(BF16)
     total[...] = score(0)
+    from_x(1, 2)
     from_core(2, range(5))
     project(2, 0, blocks)
+    total[...] += score(2)
     from_x(1, 3)
     from_x(3, 2)
-    from_z(3)
-    total[...] += score(2)
     from_core(1, range(5))
     project(1, 0, blocks)
+    total[...] += score(1)
+    from_core(3, (2,))
+    project(3, 4 * EX, 2 * B2)
+    from_z(3)
     from_x(3, 1)
-    total[...] += score(1)
+    from_x(3, 3)
     from_core(3, (0, 4))
     project(3, 0, 4 * EX)
-    from_x(3, 3)
-    from_core(3, (1, 2, 3))
-    project(3, 4 * EX, blocks - 4 * EX)
-    loads[10].wait()
+    from_core(3, (1, 3))
+    project(3, 4 * EX + 2 * B2, 2 * B1 + 2 * B2)
+    loads[9].wait()
 
     def attend(start, size):
         rows = pl.ds(pl.multiple_of(start, 16), size)
@@ -353,9 +358,11 @@
     piece_width = width // SPLIT
     sent = []
 
-    def pass_on(direction, k):
+    def pass_on(direction, k, only=None):
         position, dest = line(direction, k)
         active = last - k > position
+        if only is not None:
+            active &= position == only
         for h in range(SPLIT):
             columns = pl.ds(h * piece_width, piece_width)
             landed = from_line.at[direction, dest, h]
@@ -395,10 +402,13 @@
         swap(k)
     for k in range(1, chips):
         pair[k].wait_recv()
-        if k < last:
-            pass_on(first, k)
-    for k in range(last - (chips + 1) // 2):
-        pass_on(1 - first, k)
+
+    for step in range(1, last):
+        pass_on(first, step)
+        for i in range(1, chips // 2):
+            k = step - last + 2 * i
+            if 0 <= k < i:
+                pass_on(1 - first, k, last - i)
 
     for h in range(SPLIT):
         columns = pl.ds(h * piece_width, piece_width)

time: 80.6 us -> 81.5 us (1.011)
  the two profiles are of different devices: /device:TPU:40 before, /device:TPU:1 now
where the time goes in v3:
time: 81.5 us; the launch traced here: 81.3 us
  Pallas kernels  79.7 us (98%)
  local copies, waits for them, and re-layouts  1.57 us (2%)
    pallas_call x1, Pallas kernels, body(): pl.pallas_call(functools.partial(kernel, chips), out_shape=jax.ShapeDtype...  79.7 us

profile of v3, /device:TPU:1, one launch (start us, length us, event | category | flops | bytes accessed | tf_op | source)
XLA Modules:
  0.0 81.3 jit_solution(8792214210779739006)
XLA Ops:
  0.0 79.7 %cross_attention.1 = bf16[16,4096]{1,0:T(8,128)(2,1)} custom-call(bf16[1,288,4096]{2,1,0:T(8,128)(2,1)} %enc_ref.1, bf16[1,1,16,4096]{3,2,1,0:T(8,128)(2,1)} %dec_ref.1, bf16[4096]{0:T(1024)(128)(2,1)} %enc_gain_ref.1, bf16[1,4096]{1,0:T(2,128)(2,1)} %dec_gain_ref.1, bf16[1,4096,256]{2,1,0:T(8,128)(2,1)} %wq_ref.1, bf16[1,4096,256]{2,1,0:T(8,128)(2,1)} %wk_ref.1, ...), custom_call_target="tpu_custom_call" | custom-call | tf_op jit(solution)/shard_map/cross_attention/pallas_call | solution.py:446
  79.7 1.6 %copy.10 = bf16[1,1,16,4096]{3,2,1,0:T(8,128)(2,1)} copy(bf16[1,1,16,4096]{3,2,1,0:T(8,128)(2,1)} %bitcast.1) | data formatting | bytes 262144
